TPU v7x, 32 devices: a whole 2x2x4 slice. The times are simulated.
32 devices in a mesh: dp: 2 (over y), ctx: 4 (over z), tp: 4 (over x, core).
Axes of the slice: x: 2, y: 2, z: 4, core: 2. Of those that a mesh axis runs over, the one named last changes fastest.
Arguments:
- layer_input: bfloat16 [2, 4096, 1024], P('dp', 'ctx'), may hold values from -6 to 6
- segments: int32 [2, 4096], P('dp', 'ctx'), may hold values from 0 to 16, as said below
- positions: int32 [2, 4096], P('dp', 'ctx'), may hold values from 0 to 4094, as said below
- w_q: bfloat16 [1024, 1024], P('dp', 'tp'), may hold values from -0.1875 to 0.1875
- w_k: bfloat16 [1024, 1024], P('dp', 'tp'), may hold values from -0.1875 to 0.1875
- w_v: bfloat16 [1024, 1024], P('dp', 'tp'), may hold values from -0.1875 to 0.1875
- w_o: bfloat16 [1024, 1024], P('tp', 'dp'), may hold values from -0.75 to 0.75
- w_in: bfloat16 [1024, 4096], P('dp', 'tp'), may hold values from -0.1875 to 0.1875
- w_out: bfloat16 [4096, 1024], P('tp', 'dp'), may hold values from -0.09375 to 0.09375
- ln1_gain: bfloat16 [1024], P('dp'), may hold values from 0.25 to 1.75
- ln1_bias: bfloat16 [1024], P('dp'), may hold values from -1 to 1
- ln2_gain: bfloat16 [1024], P('dp'), may hold values from 0.25 to 1.75
- ln2_bias: bfloat16 [1024], P('dp'), may hold values from -1 to 1
- cotangent: bfloat16 [2, 4096, 1024], P('dp', 'ctx'), may hold values from -6 to 6
Outputs:
- layer_output: float32 [2, 4096, 1024], P('dp', 'ctx')
- x_grad: float32 [2, 4096, 1024], P('dp', 'ctx')
- w_q_grad: float32 [1024, 1024], P('dp', 'tp')
- w_k_grad: float32 [1024, 1024], P('dp', 'tp')
- w_v_grad: float32 [1024, 1024], P('dp', 'tp')
- w_o_grad: float32 [1024, 1024], P('tp', 'dp')
- w_in_grad: float32 [1024, 4096], P('dp', 'tp')
- w_out_grad: float32 [4096, 1024], P('tp', 'dp')
- ln1_gain_grad: float32 [1024], P('dp')
- ln1_bias_grad: float32 [1024], P('dp')
- ln2_gain_grad: float32 [1024], P('dp')
- ln2_bias_grad: float32 [1024], P('dp')
Inputs may be any that keep to these rules, and one draw needn't show every extreme that they name: `segments`: along a sequence the document number never falls; it is 0 at the first slot and 16 at the last. `positions`: A slot's position is its offset from the first slot of its document.
All inputs are finite; a program needn't handle non-finite values.
Results may differ from a plain program's by a relative error of at most 0.023.
Values may be sent and summed in bfloat16 or wider, within the bound.
No kernel may reach another device: no remote copies, remote signals or barrier semaphores. Data moves between devices by JAX's collectives and lax.ppermute only.
A program may use at most 256 MiB of HBM per device.

v0:
```python
import jax
import jax.numpy as jnp
from jax import lax
from jax.sharding import PartitionSpec as P

D = 1024
H = 16
NEG_BIG = -1e30
SQRT_HALF = 0.7071067811865476
INV_SQRT_TAU = 0.3989422804014327


def rotate_heads(values, positions, head_size, sign):
    half = head_size // 2
    freq = 10000.0 ** (-jnp.arange(half, dtype=jnp.float32) * 2.0 / head_size)
    angles = positions.astype(jnp.float32)[..., None] * freq
    cosine = jnp.cos(angles)[..., None, :]
    sine = sign * jnp.sin(angles)[..., None, :]
    first = values[..., :half]
    second = values[..., half:]
    return jnp.concatenate(
        [first * cosine - second * sine, second * cosine + first * sine], axis=-1
    )


def norm_forward(values, gain, shift):
    centered = values - jnp.mean(values, axis=-1, keepdims=True)
    inverse = lax.rsqrt(jnp.mean(centered * centered, axis=-1, keepdims=True) + 1e-05)
    normed = centered * inverse
    return (normed * gain.astype(jnp.float32) + shift.astype(jnp.float32), normed, inverse)


def norm_backward(incoming, normed, inverse, gain):
    scaled = incoming * gain.astype(jnp.float32)
    inner = (
        scaled
        - jnp.mean(scaled, axis=-1, keepdims=True)
        - normed * jnp.mean(scaled * normed, axis=-1, keepdims=True)
    )
    return (inverse * inner, jnp.sum(incoming * normed, axis=0), jnp.sum(incoming, axis=0))


def body(
    layer_input,
    segments,
    positions,
    w_q,
    w_k,
    w_v,
    w_o,
    w_in,
    w_out,
    ln1_gain,
    ln1_bias,
    ln2_gain,
    ln2_bias,
    cotangent,
):
    seqs, piece_len, width = layer_input.shape
    head_size = D // H
    (
        query_weight,
        key_weight,
        value_weight,
        out_weight,
        in_weight,
        down_weight,
        gain_one,
        shift_one,
        gain_two,
        shift_two,
    ) = (
        lax.all_gather(w_q, "dp", axis=0, tiled=True),
        lax.all_gather(w_k, "dp", axis=0, tiled=True),
        lax.all_gather(w_v, "dp", axis=0, tiled=True),
        lax.all_gather(w_o, "dp", axis=1, tiled=True),
        lax.all_gather(w_in, "dp", axis=0, tiled=True),
        lax.all_gather(w_out, "dp", axis=1, tiled=True),
        lax.all_gather(ln1_gain, "dp", axis=0, tiled=True),
        lax.all_gather(ln1_bias, "dp", axis=0, tiled=True),
        lax.all_gather(ln2_gain, "dp", axis=0, tiled=True),
        lax.all_gather(ln2_bias, "dp", axis=0, tiled=True),
    )
    local_width = query_weight.shape[1]
    heads_here = local_width // head_size
    doc_whole = lax.all_gather(segments, "ctx", axis=1, tiled=True)
    full_len = doc_whole.shape[1]
    row_count = seqs * piece_len
    tokens = layer_input.reshape(row_count, width)
    scale = head_size ** (-0.5)
    doc_low = jnp.min(segments, axis=1)
    doc_high = jnp.max(segments, axis=1)
    share = row_count // lax.axis_size("tp")
    offset = lax.axis_index("tp") * share

    def reduce_heads(partial_sum):
        return lax.psum_scatter(
            partial_sum.astype(jnp.bfloat16), "tp", scatter_dimension=0, tiled=True
        ).astype(jnp.float32)

    def spread_rows(rows_low):
        return lax.all_gather(rows_low, "tp", axis=0, tiled=True)

    def own_rows(whole_rows):
        return lax.dynamic_slice_in_dim(whole_rows, offset, share, 0)

    def project(weight):
        return jnp.dot(tokens, weight, preferred_element_type=jnp.float32).reshape(
            seqs, piece_len, heads_here, head_size
        )

    queries = rotate_heads(project(query_weight), positions, head_size, 1.0).astype(jnp.bfloat16)
    keys = rotate_heads(project(key_weight), positions, head_size, 1.0).astype(jnp.bfloat16)
    values = project(value_weight).astype(jnp.bfloat16)

    def touches():
        meets = (doc_low <= jnp.max(doc_whole, axis=1)) & (jnp.min(doc_whole, axis=1) <= doc_high)
        return (jnp.any(meets), doc_whole)

    def masked_scores(key_piece, doc_keys):
        scores = (
            jnp.einsum("sqhd,skhd->shqk", queries, key_piece, preferred_element_type=jnp.float32)
            * scale
        )
        same = segments[:, None, :, None] == doc_keys[:, None, None, :]
        return jnp.where(same, scores, NEG_BIG)

    start_state = (
        jnp.full((seqs, heads_here, piece_len), NEG_BIG, jnp.float32),
        jnp.zeros((seqs, heads_here, piece_len), jnp.float32),
        jnp.zeros((seqs, piece_len, heads_here, head_size), jnp.float32),
    )
    key_piece = lax.all_gather(keys, "ctx", axis=1, tiled=True)
    value_piece = lax.all_gather(values, "ctx", axis=1, tiled=True)
    needed, doc_keys = touches()

    def forward_update(state):
        run_max, run_total, run_out = state
        scores = masked_scores(key_piece, doc_keys)
        new_max = jnp.maximum(run_max, jnp.max(scores, axis=-1))
        weights_now = jnp.exp(scores - new_max[..., None])
        factor = jnp.exp(run_max - new_max)
        new_total = jnp.sum(weights_now, axis=-1)
        added = jnp.einsum(
            "shqk,skhd->sqhd",
            weights_now.astype(jnp.bfloat16),
            value_piece,
            preferred_element_type=jnp.float32,
        )
        new_out = run_out * jnp.swapaxes(factor, 1, 2)[..., None] + added
        return (new_max, new_total, new_out)

    run_max, run_total, run_out = lax.cond(needed, forward_update, lambda state: state, start_state)
    attended = run_out / jnp.swapaxes(run_total, 1, 2)[..., None]
    log_total = run_max + jnp.log(run_total)
    attended_low = attended.astype(jnp.bfloat16).reshape(row_count, local_width)
    mixed = reduce_heads(jnp.dot(attended_low, out_weight, preferred_element_type=jnp.float32))
    token_rows = own_rows(tokens).astype(jnp.float32)
    hidden_one, normed_one, inverse_one = norm_forward(token_rows + mixed, gain_one, shift_one)
    hidden_low = spread_rows(hidden_one.astype(jnp.bfloat16))
    pre_act = jnp.dot(hidden_low, in_weight, preferred_element_type=jnp.float32)
    activated = jax.nn.gelu(pre_act, approximate=False).astype(jnp.bfloat16)
    branch_two = reduce_heads(jnp.dot(activated, down_weight, preferred_element_type=jnp.float32))
    output, normed_two, inverse_two = norm_forward(hidden_one + branch_two, gain_two, shift_two)
    out_grad = own_rows(cotangent.reshape(row_count, width)).astype(jnp.float32)
    second_grad, gain_two_grad, shift_two_grad = norm_backward(
        out_grad, normed_two, inverse_two, gain_two
    )
    second_low = spread_rows(second_grad.astype(jnp.bfloat16))
    down_grad = jnp.einsum("rf,rd->fd", activated, second_low, preferred_element_type=jnp.float32)
    act_grad = jnp.einsum("rd,fd->rf", second_low, down_weight, preferred_element_type=jnp.float32)
    slope = (
        0.5 * (1.0 + jax.scipy.special.erf(pre_act * SQRT_HALF))
        + pre_act * jnp.exp(-0.5 * pre_act * pre_act) * INV_SQRT_TAU
    )
    pre_grad = (act_grad * slope).astype(jnp.bfloat16)
    in_grad = jnp.einsum("rd,rf->df", hidden_low, pre_grad, preferred_element_type=jnp.float32)
    hidden_grad = second_grad + reduce_heads(
        jnp.einsum("rf,df->rd", pre_grad, in_weight, preferred_element_type=jnp.float32)
    )
    first_grad, gain_one_grad, shift_one_grad = norm_backward(
        hidden_grad, normed_one, inverse_one, gain_one
    )
    first_low = spread_rows(first_grad.astype(jnp.bfloat16))
    out_weight_grad = jnp.einsum(
        "rj,rd->jd", attended_low, first_low, preferred_element_type=jnp.float32
    )
    heads_grad = jnp.einsum("rd,jd->rj", first_low, out_weight, preferred_element_type=jnp.float32)
    heads_grad = heads_grad.astype(jnp.bfloat16).reshape(seqs, piece_len, heads_here, head_size)
    row_dot = jnp.swapaxes(jnp.sum(heads_grad.astype(jnp.float32) * attended, axis=-1), 1, 2)
    back_state = (
        jnp.zeros((seqs, piece_len, heads_here, head_size), jnp.float32),
        jnp.zeros((seqs, full_len, heads_here, head_size), jnp.float32),
        jnp.zeros((seqs, full_len, heads_here, head_size), jnp.float32),
    )
    backward_key_piece = lax.all_gather(keys, "ctx", axis=1, tiled=True)
    backward_value_piece = lax.all_gather(values, "ctx", axis=1, tiled=True)
    needed, backward_doc_keys = touches()

    def backward_update(state):
        scores = masked_scores(backward_key_piece, backward_doc_keys)
        probs = jnp.exp(scores - log_total[..., None])
        value_part = jnp.einsum(
            "shqk,sqhd->skhd",
            probs.astype(jnp.bfloat16),
            heads_grad,
            preferred_element_type=jnp.float32,
        )
        prob_grad = jnp.einsum(
            "sqhd,skhd->shqk", heads_grad, backward_value_piece, preferred_element_type=jnp.float32
        )
        score_grad = (probs * (prob_grad - row_dot[..., None])).astype(jnp.bfloat16)
        query_grad = (
            jnp.einsum(
                "shqk,skhd->sqhd",
                score_grad,
                backward_key_piece,
                preferred_element_type=jnp.float32,
            )
            * scale
        )
        key_part = (
            jnp.einsum("shqk,sqhd->skhd", score_grad, queries, preferred_element_type=jnp.float32)
            * scale
        )
        return (query_grad, key_part, value_part)

    query_grad, key_grad_all, value_grad_all = lax.cond(
        needed, backward_update, lambda state: state, back_state
    )
    key_grad, value_grad = (
        lax.psum_scatter(
            key_grad_all.astype(jnp.bfloat16), "ctx", scatter_dimension=1, tiled=True
        ).astype(jnp.float32),
        lax.psum_scatter(
            value_grad_all.astype(jnp.bfloat16), "ctx", scatter_dimension=1, tiled=True
        ).astype(jnp.float32),
    )
    query_low = (
        rotate_heads(query_grad, positions, head_size, -1.0)
        .astype(jnp.bfloat16)
        .reshape(row_count, local_width)
    )
    key_low = (
        rotate_heads(key_grad, positions, head_size, -1.0)
        .astype(jnp.bfloat16)
        .reshape(row_count, local_width)
    )
    value_low = value_grad.astype(jnp.bfloat16).reshape(row_count, local_width)
    query_weight_grad = jnp.einsum(
        "rd,rj->dj", tokens, query_low, preferred_element_type=jnp.float32
    )
    key_weight_grad = jnp.einsum("rd,rj->dj", tokens, key_low, preferred_element_type=jnp.float32)
    value_weight_grad = jnp.einsum(
        "rd,rj->dj", tokens, value_low, preferred_element_type=jnp.float32
    )
    input_part = jnp.einsum(
        "rj,dj->rd", query_low, query_weight, preferred_element_type=jnp.float32
    )
    input_part = input_part + jnp.einsum(
        "rj,dj->rd", key_low, key_weight, preferred_element_type=jnp.float32
    )
    input_part = input_part + jnp.einsum(
        "rj,dj->rd", value_low, value_weight, preferred_element_type=jnp.float32
    )
    input_grad = first_grad + reduce_heads(input_part)
    norm_terms = jnp.stack([gain_one_grad, shift_one_grad, gain_two_grad, shift_two_grad])[None]
    output, input_grad, norm_terms = (
        lax.all_gather(output.astype(jnp.bfloat16), "tp", axis=0, tiled=True).astype(output.dtype),
        lax.all_gather(input_grad.astype(jnp.bfloat16), "tp", axis=0, tiled=True).astype(
            input_grad.dtype
        ),
        lax.all_gather(norm_terms.astype(jnp.bfloat16), "tp", axis=0, tiled=True).astype(
            norm_terms.dtype
        ),
    )
    norm_terms = jnp.sum(norm_terms, axis=0)
    gain_one_grad, shift_one_grad, gain_two_grad, shift_two_grad = (
        norm_terms[0],
        norm_terms[1],
        norm_terms[2],
        norm_terms[3],
    )
    shares = (
        lax.psum_scatter(
            query_weight_grad.astype(jnp.bfloat16), "dp", scatter_dimension=0, tiled=True
        ).astype(jnp.float32),
        lax.psum_scatter(
            key_weight_grad.astype(jnp.bfloat16), "dp", scatter_dimension=0, tiled=True
        ).astype(jnp.float32),
        lax.psum_scatter(
            value_weight_grad.astype(jnp.bfloat16), "dp", scatter_dimension=0, tiled=True
        ).astype(jnp.float32),
        lax.psum_scatter(
            out_weight_grad.astype(jnp.bfloat16), "dp", scatter_dimension=1, tiled=True
        ).astype(jnp.float32),
        lax.psum_scatter(
            in_grad.astype(jnp.bfloat16), "dp", scatter_dimension=0, tiled=True
        ).astype(jnp.float32),
        lax.psum_scatter(
            down_grad.astype(jnp.bfloat16), "dp", scatter_dimension=1, tiled=True
        ).astype(jnp.float32),
        lax.psum_scatter(
            gain_one_grad.astype(jnp.bfloat16), "dp", scatter_dimension=0, tiled=True
        ).astype(jnp.float32),
        lax.psum_scatter(
            shift_one_grad.astype(jnp.bfloat16), "dp", scatter_dimension=0, tiled=True
        ).astype(jnp.float32),
        lax.psum_scatter(
            gain_two_grad.astype(jnp.bfloat16), "dp", scatter_dimension=0, tiled=True
        ).astype(jnp.float32),
        lax.psum_scatter(
            shift_two_grad.astype(jnp.bfloat16), "dp", scatter_dimension=0, tiled=True
        ).astype(jnp.float32),
    )
    totals = (
        lax.psum(shares[0].astype(jnp.bfloat16), "ctx").astype(jnp.float32),
        lax.psum(shares[1].astype(jnp.bfloat16), "ctx").astype(jnp.float32),
        lax.psum(shares[2].astype(jnp.bfloat16), "ctx").astype(jnp.float32),
        lax.psum(shares[3].astype(jnp.bfloat16), "ctx").astype(jnp.float32),
        lax.psum(shares[4].astype(jnp.bfloat16), "ctx").astype(jnp.float32),
        lax.psum(shares[5].astype(jnp.bfloat16), "ctx").astype(jnp.float32),
        lax.psum(shares[6].astype(jnp.bfloat16), "ctx").astype(jnp.float32),
        lax.psum(shares[7].astype(jnp.bfloat16), "ctx").astype(jnp.float32),
        lax.psum(shares[8].astype(jnp.bfloat16), "ctx").astype(jnp.float32),
        lax.psum(shares[9].astype(jnp.bfloat16), "ctx").astype(jnp.float32),
    )
    return (
        output.reshape(seqs, piece_len, width),
        input_grad.reshape(seqs, piece_len, width),
        totals[0],
        totals[1],
        totals[2],
        totals[3],
        totals[4],
        totals[5],
        totals[6],
        totals[7],
        totals[8],
        totals[9],
    )


def solution(mesh):
    return jax.shard_map(
        body,
        mesh=mesh,
        in_specs=(
            P("dp", "ctx", None),
            P("dp", "ctx"),
            P("dp", "ctx"),
            P("dp", "tp"),
            P("dp", "tp"),
            P("dp", "tp"),
            P("tp", "dp"),
            P("dp", "tp"),
            P("tp", "dp"),
            P("dp"),
            P("dp"),
            P("dp"),
            P("dp"),
            P("dp", "ctx", None),
        ),
        out_specs=(
            P("dp", "ctx", None),
            P("dp", "ctx", None),
            P("dp", "tp"),
            P("dp", "tp"),
            P("dp", "tp"),
            P("tp", "dp"),
            P("dp", "tp"),
            P("tp", "dp"),
            P("dp"),
            P("dp"),
            P("dp"),
            P("dp"),
        ),
        check_vma=False,
    )
```

profile of v0, /device:TPU:0, one launch (start us, length us, event | category | flops | bytes accessed | tf_op | source)
XLA Modules:
  0.0 972.7 jit_solution(8596426434265717203)
XLA Ops:
  8.1 10.4 %all_gather.63 = bf16[1024,256]{1,0:T(8,128)(2,1)S(1)} all-gather(bf16[512,256]{1,0:T(8,128)(2,1)} %param.23), channel_id=1, replica_groups=mesh['dp'=2,'ctx'=4,'tp'=4] {'dp'}, dimensions={0}, use_global_device_ids=true | all-gather | bytes 786432 | tf_op jit(solution)/shard_map/all_gather | solution.py:75
  18.7 3.2 fusion.94
  21.9 8.1 all_gather.61
  30.3 7.3 all_gather.60
  39.0 2.4 fusion.79
  41.4 2.4 fusion.76
  45.1 13.8 %all_gather.59 = s32[1,4096]{1,0:T(1,128)S(1)} all-gather(s32[1,1024]{1,0:T(1,128)S(1)} %copy-done.25), channel_id=1, replica_groups=mesh['dp'=2,'ctx'=4,'tp'=4] {'ctx'}, dimensions={1}, use_global_device_ids=true | all-gather | bytes 20480 | tf_op jit(solution)/shard_map/all_gather | solution.py:86
  62.8 7.0 all_gather.65
  69.8 46.2 %all-gather.15.cloned.1.call-done = bf16[1,4096,4,64]{1,3,2,0:T(8,128)(2,1)} async-done(((bf16[1,1024,4,64]{1,3,2,0:T(8,128)(2,1)}), bf16[1,4096,4,64]{1,3,2,0:T(8,128)(2,1)}) %all-gather.15.cloned.1.call-update) | async-done | bytes 2097168 | tf_op jit(solution)/shard_map/all_gather | solution.py:133
  116.0 81.0 %conditional.2 = (f32[1,4,1024]{2,1,0:T(4,128)S(1)}, f32[1,4,1024]{2,1,0:T(4,128)}, f32[1,1024,4,64]{1,3,2,0:T(8,128)S(1)}, f32[1,4,1024]{2,1,0:T(4,128)S(1)}) conditional(s32[]{:T(128)} %convert_element_type.302, () %tuple.32, (s32[1,1024]{1,0:T(1,128)S(1)}, s32[1,4096]{1,0:T(1,128)S(1)}, bf16[1,1024,4,64]{1,3,2,0:T(8,128)(2,1)S(1)}, ...), branch_computations={%region_4.0_spmd, %region_5.8_spmd} | conditional | flops 4483981312 | bytes 232476736 | solution.py:153
  116.2 4.7 broadcast_compare_fusion
  120.9 25.9 %fusion = (f32[4,1024]{1,0:T(4,128)S(1)}, f32[4,1024,4096]{2,1,0:T(8,128)}) fusion(pred[1024,4096]{1,0:T(8,128)(4,1)} %broadcast_compare_fusion, bf16[1,4096,4,64]{1,3,2,0:T(8,128)(2,1)S(1)} %copy-done.2, bf16[1,1024,4,64]{1,3,2,0:T(8,128)(2,1)S(1)} %get-tuple-element.51), kind=kOutput, calls=%fused_computation.2 | convolution fusion | flops 2197811200 | bytes 73940992 | tf_op jit(solution)/shard_map/cond/branch_1_fun/sqhd,skhd->shqk/dot_general | solution.py:122
  146.8 23.3 %fusion.2 = f32[4,1024]{1,0:T(4,128)} fusion(f32[4,1024,4096]{2,1,0:T(8,128)} %get-tuple-element.155, f32[4,1024]{1,0:T(4,128)S(1)} %broadcast_maximum_fusion, pred[1024,4096]{1,0:T(8,128)(4,1)} %broadcast_compare_fusion), kind=kLoop, calls=%fused_computation.4 | loop fusion | flops 67104768 | bytes 71335936 | tf_op jit(solution)/shard_map/cond/branch_1_fun/reduce_sum | solution.py:143
  170.9 26.1 %fusion.14 = f32[1,1024,4,64]{1,3,2,0:T(8,128)S(1)} fusion(bf16[1,4096,4,64]{1,3,2,0:T(8,128)(2,1)} %get-tuple-element.53, f32[4,1024,4096]{2,1,0:T(8,128)} %get-tuple-element.155, f32[4,1024]{1,0:T(4,128)S(1)} %broadcast_maximum_fusion, pred[1024,4096]{1,0:T(8,128)(4,1)} %broadcast_compare_fusion, f32[1024,4]{0,1:T(4,128)S(1)} %get-tuple-element.144), kind=kOutput, calls=%fused_computation.12 | convolution fusion | flops 2214854656 | bytes 74481664 | tf_op jit(solution)/shard_map/cond/branch_1_fun/shqk,skhd->sqhd/dot_general | solution.py:144
  201.4 4.4 all-gather.1
  205.8 4.4 all-gather.2
  210.2 20.7 %reduce-scatter.13.cloned.1.call-done = bf16[256,1024]{1,0:T(8,128)(2,1)} async-done(((bf16[1024,1024]{1,0:T(8,128)(2,1)}), bf16[256,1024]{1,0:T(8,128)(2,1)}) %reduce-scatter.13.cloned.1.call-update) | async-done | bytes 524304 | tf_op jit(solution)/shard_map/reduce_scatter | solution.py:97
  233.8 2.3 fusion.113
  236.8 22.2 %all-gather.17.cloned.1.call-done = bf16[1024,1024]{1,0:T(8,128)(2,1)} async-done(((bf16[256,1024]{1,0:T(8,128)(2,1)}), bf16[1024,1024]{1,0:T(8,128)(2,1)}) %all-gather.17.cloned.1.call-update) | async-done | bytes 2097168 | tf_op jit(solution)/shard_map/all_gather | solution.py:102
  259.1 14.3 %fusion.50 = (bf16[1024,1024]{1,0:T(8,128)(2,1)}, f32[1024,1024]{1,0:T(8,128)}) fusion(bf16[1024,1024]{1,0:T(8,128)(2,1)} %all-gather.17.cloned.1.call-done, bf16[1024,1024]{1,0:T(8,128)(2,1)} %all-gather.19.cloned.1.call-done), kind=kOutput, calls=%fused_computation.46 | convolution fusion | flops 2215641088 | bytes 10485760 | tf_op jit(solution)/shard_map/dot_general | solution.py:161
  273.4 20.1 %all-gather.21.cloned.1.call-done = bf16[1024,1024]{1,0:T(8,128)(2,1)} async-done(((bf16[1024,512]{1,0:T(8,128)(2,1)}), bf16[1024,1024]{1,0:T(8,128)(2,1)}) %all-gather.21.cloned.1.call-update) | async-done | bytes 2097168 | tf_op jit(solution)/shard_map/all_gather | solution.py:78
  293.5 5.9 convolution_convert_fusion.3
  299.5 4.4 all-gather.3
  303.9 4.4 all-gather.4
  308.3 22.5 %reduce-scatter.15.cloned.1.call-done = bf16[256,1024]{1,0:T(8,128)(2,1)} async-done(((bf16[1024,1024]{1,0:T(8,128)(2,1)}), bf16[256,1024]{1,0:T(8,128)(2,1)}) %reduce-scatter.15.cloned.1.call-update) | async-done | bytes 524304 | tf_op jit(solution)/shard_map/reduce_scatter | solution.py:97
  332.7 2.1 fusion.109
  334.8 2.5 fusion.120
  337.5 22.5 %all-gather.25.cloned.1.call-done = bf16[1024,1024]{1,0:T(8,128)(2,1)} async-done(((bf16[256,1024]{1,0:T(8,128)(2,1)}), bf16[1024,1024]{1,0:T(8,128)(2,1)}) %all-gather.25.cloned.1.call-update) | async-done | bytes 2097168 | tf_op jit(solution)/shard_map/all_gather | solution.py:102
  360.0 6.3 fusion.56
  367.7 3.7 convolution_convert_fusion.2
  371.5 31.3 %reduce-scatter.17.cloned.1.call-done = bf16[256,1024]{1,0:T(8,128)(2,1)} async-done(((bf16[1024,1024]{1,0:T(8,128)(2,1)}), bf16[256,1024]{1,0:T(8,128)(2,1)}) %reduce-scatter.17.cloned.1.call-update) | async-done | bytes 524304 | tf_op jit(solution)/shard_map/reduce_scatter | solution.py:97
  402.8 2.4 multiply_reduce_fusion
  405.2 2.8 fusion.119
  408.0 22.7 %all-gather.27.cloned.1.call-done = bf16[1024,1024]{1,0:T(8,128)(2,1)} async-done(((bf16[256,1024]{1,0:T(8,128)(2,1)}), bf16[1024,1024]{1,0:T(8,128)(2,1)}) %all-gather.27.cloned.1.call-update) | async-done | bytes 2097168 | tf_op jit(solution)/shard_map/all_gather | solution.py:102
  430.7 2.6 convolution_convert_fusion.6
  434.2 129.8 %conditional.3 = (bf16[1,4096,4,64]{1,3,2,0:T(8,128)(2,1)}, bf16[1,4096,4,64]{1,3,2,0:T(8,128)(2,1)}, f32[1,1024,4,32]{1,3,2,0:T(8,128)}, f32[1,1024,4,32]{1,3,2,0:T(8,128)S(1)}) conditional(s32[]{:T(128)} %convert_element_type.302, () %tuple.34, (s32[1,1024]{1,0:T(1,128)S(1)}, s32[1,4096]{1,0:T(1,128)S(1)}, ...), branch_computations={%region_20.21_spmd, %region_21.22_spmd} | conditional | flops 10911748096 | bytes 349294720 | solution.py:228
  434.3 4.7 broadcast_compare_fusion.1
  439.0 23.1 %fusion.34 = f32[4,1024,4096]{2,1,0:T(8,128)} fusion(bf16[1,4096,4,64]{1,3,2,0:T(8,128)(2,1)S(1)} %get-tuple-element.57, bf16[1,1024,4,64]{1,3,2,0:T(8,128)(2,1)S(1)} %get-tuple-element.56), kind=kOutput, calls=%fused_computation.31 | convolution fusion | flops 2147483648 | bytes 69730304 | tf_op jit(solution)/shard_map/cond/branch_1_fun/sqhd,skhd->shqk/dot_general | solution.py:122
  462.2 28.2 %fusion.28 = bf16[1,4096,4,64]{1,3,2,0:T(8,128)(2,1)} fusion(f32[4,1024,4096]{2,1,0:T(8,128)} %fusion.34, f32[4,1024]{1,0:T(4,128)S(1)} %add_bitcast_fusion, pred[1024,4096]{1,0:T(8,128)(4,1)} %broadcast_compare_fusion.1, bf16[1,1024,4,64]{1,3,2,0:T(8,128)(2,1)S(1)} %get-tuple-element.60), kind=kOutput, calls=%fused_computation.27 | convolution fusion | flops 2214592512 | bytes 73940992 | tf_op jit(solution)/shard_map/cond/branch_1_fun/shqk,sqhd->skhd/dot_general | solution.py:203
  490.3 41.9 %multiply_convert_fusion = bf16[4,1024,4096]{2,1,0:T(8,128)(2,1)} fusion(f32[4,1024,4096]{2,1,0:T(8,128)} %fusion.34, f32[4,1024]{1,0:T(4,128)S(1)} %bitcast.238, f32[4,1024]{1,0:T(4,128)S(1)} %add_bitcast_fusion, pred[1024,4096]{1,0:T(8,128)(4,1)} %broadcast_compare_fusion.1, bf16[1,4096,4,64]{1,3,2,0:T(8,128)(2,1)} %get-tuple-element.61, ...), kind=kOutput, calls=%fused_computation.19 | convolution fusion | flops 2248146944 | bytes 107511808 | tf_op jit(solution)/shard_map/cond/branch_1_fun/sqhd,skhd->shqk/dot_general | solution.py:209
  532.2 15.6 %fusion.39 = f32[1,1024,4,64]{1,3,2,0:T(8,128)S(1)} fusion(bf16[4,1024,4096]{2,1,0:T(8,128)(2,1)} %multiply_convert_fusion, bf16[1,4096,4,64]{1,3,2,0:T(8,128)(2,1)S(1)} %copy-done.4), kind=kOutput, calls=%fused_computation.34 | convolution fusion | flops 2147745792 | bytes 36700160 | tf_op jit(solution)/shard_map/cond/branch_1_fun/shqk,skhd->sqhd/dot_general | solution.py:214
  547.8 15.1 %fusion.27 = bf16[1,4096,4,64]{1,3,2,0:T(8,128)(2,1)} fusion(bf16[4,1024,4096]{2,1,0:T(8,128)(2,1)} %multiply_convert_fusion, bf16[1,1024,4,64]{1,3,2,0:T(8,128)(2,1)S(1)} %get-tuple-element.56), kind=kOutput, calls=%fused_computation.26 | convolution fusion | flops 2149580800 | bytes 36175872 | tf_op jit(solution)/shard_map/cond/branch_1_fun/shqk,sqhd->skhd/dot_general | solution.py:223
  565.6 5.3 convolution_convert_fusion.1
  571.0 6.0 convolution_convert_fusion
  577.1 3.2 convolution_convert_fusion.5
  580.4 27.4 %reduce-scatter.21.cloned.1.call-done = bf16[1,1024,4,64]{1,3,2,0:T(8,128)(2,1)} async-done(((bf16[1,4096,4,64]{1,3,2,0:T(8,128)(2,1)}), bf16[1,1024,4,64]{1,3,2,0:T(8,128)(2,1)}) %reduce-scatter.21.cloned.1.call-update) | async-done | bytes 524304 | tf_op jit(solution)/shard_map/reduce_scatter | solution.py:235
  607.8 2.5 fusion.100
  610.4 43.1 %reduce-scatter.19.cloned.1.call-done = bf16[1,1024,4,64]{1,3,2,0:T(8,128)(2,1)} async-done(((bf16[1,4096,4,64]{1,3,2,0:T(8,128)(2,1)}), bf16[1,1024,4,64]{1,3,2,0:T(8,128)(2,1)}) %reduce-scatter.19.cloned.1.call-update) | async-done | bytes 524304 | tf_op jit(solution)/shard_map/reduce_scatter | solution.py:232
  656.2 3.2 fusion.97
  659.4 3.2 fusion.103
  667.2 20.3 %reduce-scatter.33.cloned.1.call-done = bf16[512,1024]{1,0:T(8,128)(2,1)} async-done(((bf16[1024,1024]{1,0:T(8,128)(2,1)}), bf16[512,1024]{1,0:T(8,128)(2,1)}) %reduce-scatter.33.cloned.1.call-update) | async-done | bytes 1048592 | tf_op jit(solution)/shard_map/reduce_scatter | solution.py:297
  687.5 34.2 %reduce-scatter.35.cloned.1.call-done = bf16[1024,512]{1,0:T(8,128)(2,1)} async-done(((bf16[1024,1024]{1,0:T(8,128)(2,1)}), bf16[1024,512]{1,0:T(8,128)(2,1)}) %reduce-scatter.35.cloned.1.call-update) | async-done | bytes 1048592 | tf_op jit(solution)/shard_map/reduce_scatter | solution.py:300
  721.7 16.8 %reduce-scatter.31.cloned.1.call-done = bf16[256,512]{1,0:T(8,128)(2,1)} async-done(((bf16[256,1024]{1,0:T(8,128)(2,1)}), bf16[256,512]{1,0:T(8,128)(2,1)}) %reduce-scatter.31.cloned.1.call-update) | async-done | bytes 262160 | tf_op jit(solution)/shard_map/reduce_scatter | solution.py:294
  738.5 17.5 %reduce-scatter.29.cloned.1.call-done = bf16[512,256]{0,1:T(8,128)(2,1)} async-done(((bf16[1024,256]{0,1:T(8,128)(2,1)}), bf16[512,256]{0,1:T(8,128)(2,1)}) %reduce-scatter.29.cloned.1.call-update) | async-done | bytes 262160 | tf_op jit(solution)/shard_map/reduce_scatter | solution.py:291
  756.0 17.3 %reduce-scatter.27.cloned.1.call-done = bf16[512,256]{0,1:T(8,128)(2,1)} async-done(((bf16[1024,256]{0,1:T(8,128)(2,1)}), bf16[512,256]{0,1:T(8,128)(2,1)}) %reduce-scatter.27.cloned.1.call-update) | async-done | bytes 262160 | tf_op jit(solution)/shard_map/reduce_scatter | solution.py:288
  773.3 17.5 %reduce-scatter.25.cloned.1.call-done = bf16[512,256]{0,1:T(8,128)(2,1)} async-done(((bf16[1024,256]{0,1:T(8,128)(2,1)}), bf16[512,256]{0,1:T(8,128)(2,1)}) %reduce-scatter.25.cloned.1.call-update) | async-done | bytes 262160 | tf_op jit(solution)/shard_map/reduce_scatter | solution.py:285
  790.9 34.1 %reduce-scatter.23.cloned.1.call-done = bf16[256,1024]{1,0:T(8,128)(2,1)} async-done(((bf16[1024,1024]{1,0:T(8,128)(2,1)}), bf16[256,1024]{1,0:T(8,128)(2,1)}) %reduce-scatter.23.cloned.1.call-update) | async-done | bytes 524304 | tf_op jit(solution)/shard_map/reduce_scatter | solution.py:97
  829.5 4.4 bitcast_convert_fusion.1
  833.9 5.3 all_gather.77
  839.3 5.0 all-reduce.6
  844.6 12.0 %all-reduce.4 = (bf16[512]{0:T(512)(128)(2,1)S(1)}, bf16[512]{0:T(512)(128)(2,1)S(1)}, bf16[512]{0:T(512)(128)(2,1)S(1)}, bf16[512]{0:T(512)(128)(2,1)S(1)}) all-reduce(bf16[512]{0:T(512)(128)(2,1)S(1)} %dynamic-slice.3, bf16[512]{0:T(512)(128)(2,1)S(1)} %dynamic-slice.5, ...), channel_id=1, replica_groups=mesh['dp'=2,'ctx'=4,'tp'=4] {'ctx'}, use_global_device_ids=true, to_apply=%region_43.44 | all-reduce | flops 2048 | bytes 8192 | tf_op jit(solution)/shard_map/psum | solution.py:323
  859.0 90.2 %all-reduce.9.cloned.1.call-done = (bf16[512,256]{0,1:T(8,128)(2,1)}, bf16[512,256]{0,1:T(8,128)(2,1)}, bf16[512,256]{0,1:T(8,128)(2,1)}, bf16[256,512]{1,0:T(8,...) async-done(((bf16[512,256]{0,1:T(8,128)(2,1)}, bf16[512,256]{0,1:T(8,128)(2,1)}, bf16[512,256]{0,1:T(8,128)(2,1)}, bf16[256,512]{1,0:T(8,128)(2,1)}, ...) | async-done | bytes 3145744 | tf_op jit(solution)/shard_map/psum | solution.py:317
  956.7 2.8 convert_element_type.349
  961.1 4.1 bitcast_convert_fusion
  (192 shorter events, 43.4 us)
Async XLA Ops:
  8.0 13.9 %copy-start.29 = (s32[1,1024]{1,0:T(1,128)S(1)}, s32[1,1024]{1,0:T(1,128)}, u32[]{:S(2)}) copy-start(s32[1,1024]{1,0:T(1,128)} %param.20) | copy-start | bytes 12292
  8.0 13.9 %copy-start.22 = (bf16[512,256]{1,0:T(8,128)(2,1)S(1)}, bf16[512,256]{1,0:T(8,128)(2,1)}, u32[]{:S(2)}) copy-start(bf16[512,256]{1,0:T(8,128)(2,1)} %param.22) | copy-start | bytes 786436
  8.0 61.8 %all-gather.31.cloned.1.call-start = ((), (), s32[]{:S(2)}) async-start(), calls=%async_computation.32 | async-start | bytes 2621440 | tf_op jit(solution)/shard_map/all_gather | solution.py:134
  18.4 11.9 %copy-start.5 = (bf16[1024,256]{1,0:T(8,128)(2,1)}, bf16[1024,256]{1,0:T(8,128)(2,1)S(1)}, u32[]{:S(2)}) copy-start(bf16[1024,256]{1,0:T(8,128)(2,1)S(1)} %all_gather.63) | copy-start | bytes 1572868
  18.4 11.9 %copy-start.23 = (bf16[512,256]{1,0:T(8,128)(2,1)S(1)}, bf16[512,256]{1,0:T(8,128)(2,1)}, u32[]{:S(2)}) copy-start(bf16[512,256]{1,0:T(8,128)(2,1)} %param.21) | copy-start | bytes 786436
  21.9 94.1 %all-gather.15.cloned.1.call-start = ((), (), s32[]{:S(2)}) async-start(), calls=%async_computation.12 | async-start | bytes 2621440 | tf_op jit(solution)/shard_map/all_gather | solution.py:133
  30.1 13.7 %copy-start.7 = (bf16[1024,256]{1,0:T(8,128)(2,1)}, bf16[1024,256]{1,0:T(8,128)(2,1)S(1)}, u32[]{:S(2)}) copy-start(bf16[1024,256]{1,0:T(8,128)(2,1)S(1)} %all_gather.61) | copy-start | bytes 1572868
  37.6 6.2 copy-start.9
  39.0 4.8 copy-start.16
  41.4 3.7 copy-start.25
  43.8 19.0 %copy-start.24 = (bf16[256,512]{1,0:T(8,128)(2,1)S(1)}, bf16[256,512]{1,0:T(8,128)(2,1)}, u32[]{:S(2)}) copy-start(bf16[256,512]{1,0:T(8,128)(2,1)} %param.24) | copy-start | bytes 786436
  45.0 185.9 %reduce-scatter.13.cloned.1.call-start = ((), (), s32[]{:S(2)}) async-start(), calls=%async_computation.13 | async-start | bytes 2621440 | tf_op jit(solution)/shard_map/reduce_scatter | solution.py:97
  69.8 128.1 %copy-start.15 = (bf16[256,1024]{1,0:T(8,128)(2,1)}, bf16[256,1024]{1,0:T(8,128)(2,1)S(1)}, u32[]{:S(2)}) copy-start(bf16[256,1024]{1,0:T(8,128)(2,1)S(1)} %all_gather.65) | copy-start | bytes 1572868
  116.2 4.8 copy-start.2
  197.0 4.4 copy-start.30
  197.0 8.8 copy-start.31
  197.9 0.8 copy-start.13
  200.8 36.0 %all-gather.19.cloned.1.call-start = ((), (), s32[]{:S(2)}) async-start(), calls=%async_computation.15 | async-start | bytes 3145728 | tf_op jit(solution)/shard_map/all_gather | solution.py:77
  201.4 57.7 %all-gather.17.cloned.1.call-start = ((), (), s32[]{:S(2)}) async-start(), calls=%async_computation.14 | async-start | bytes 2621440 | tf_op jit(solution)/shard_map/all_gather | solution.py:102
  236.1 57.3 %all-gather.21.cloned.1.call-start = ((), (), s32[]{:S(2)}) async-start(), calls=%async_computation.16 | async-start | bytes 3145728 | tf_op jit(solution)/shard_map/all_gather | solution.py:78
  236.7 94.0 %reduce-scatter.15.cloned.1.call-start = ((), (), s32[]{:S(2)}) async-start(), calls=%async_computation.17 | async-start | bytes 2621440 | tf_op jit(solution)/shard_map/reduce_scatter | solution.py:97
  293.5 6.0 copy-start.32
  293.5 10.4 %copy-start.33 = (bf16[512]{0:T(512)(128)(2,1)S(1)}, bf16[512]{0:T(512)(128)(2,1)}, u32[]{:S(2)}) copy-start(bf16[512]{0:T(512)(128)(2,1)} %param.30) | copy-start | bytes 3076
  293.5 37.3 %copy-start = (bf16[256,1024]{1,0:T(8,128)(2,1)S(1)}, bf16[256,1024]{1,0:T(8,128)(2,1)}, u32[]{:S(2)}) copy-start(bf16[256,1024]{1,0:T(8,128)(2,1)} %reduce-scatter.13.cloned.1.call-done) | copy-start | bytes 1572868
  299.4 60.6 %all-gather.25.cloned.1.call-start = ((), (), s32[]{:S(2)}) async-start(), calls=%async_computation.19 | async-start | bytes 2621440 | tf_op jit(solution)/shard_map/all_gather | solution.py:102
  337.3 65.5 %reduce-scatter.17.cloned.1.call-start = ((), (), s32[]{:S(2)}) async-start(), calls=%async_computation.20 | async-start | bytes 2621440 | tf_op jit(solution)/shard_map/reduce_scatter | solution.py:97
  360.0 7.7 copy-start.35
  366.4 1.3 copy-start.37
  371.5 59.3 %all-gather.27.cloned.1.call-start = ((), (), s32[]{:S(2)}) async-start(), calls=%async_computation.21 | async-start | bytes 2621440 | tf_op jit(solution)/shard_map/all_gather | solution.py:102
  408.0 199.8 %reduce-scatter.21.cloned.1.call-start = ((), (), s32[]{:S(2)}) async-start(), calls=%async_computation.23 | async-start | bytes 2621440 | tf_op jit(solution)/shard_map/reduce_scatter | solution.py:235
  430.7 3.5 copy-start.1
  434.2 4.8 copy-start.3
  434.3 27.9 %copy-start.20 = (bf16[1,1024,4,64]{1,3,2,0:T(8,128)(2,1)}, bf16[1,1024,4,64]{1,3,2,0:T(8,128)(2,1)S(1)}, u32[]{:S(2)}) copy-start(bf16[1,1024,4,64]{1,3,2,0:T(8,128)(2,1)S(1)} %get-tuple-element.60) | copy-start | bytes 1572868 | tf_op jit(solution)/shard_map/cond
  490.3 41.9 %copy-start.4 = (bf16[1,4096,4,64]{1,3,2,0:T(8,128)(2,1)S(1)}, bf16[1,4096,4,64]{1,3,2,0:T(8,128)(2,1)}, u32[]{:S(2)}) copy-start(bf16[1,4096,4,64]{1,3,2,0:T(8,128)(2,1)} %copy-done.3) | copy-start | bytes 6291460 | tf_op jit(solution)/shard_map/cond
  564.0 1.6 copy-start.34
  564.0 89.5 %reduce-scatter.19.cloned.1.call-start = ((), (), s32[]{:S(2)}) async-start(), calls=%async_computation.22 | async-start | bytes 2621440 | tf_op jit(solution)/shard_map/reduce_scatter | solution.py:232
  564.8 122.7 %reduce-scatter.33.cloned.1.call-start = ((), (), s32[]{:S(2)}) async-start(), calls=%async_computation.30 | async-start | bytes 3145728 | tf_op jit(solution)/shard_map/reduce_scatter | solution.py:297
  570.9 6.1 copy-start.14
  570.9 150.8 %reduce-scatter.35.cloned.1.call-start = ((), (), s32[]{:S(2)}) async-start(), calls=%async_computation.31 | async-start | bytes 3145728 | tf_op jit(solution)/shard_map/reduce_scatter | solution.py:300
  577.0 30.9 %copy-start.11 = (bf16[1,1024,1024]{2,1,0:T(8,128)(2,1)S(1)}, bf16[1,1024,1024]{2,1,0:T(8,128)(2,1)}, u32[]{:S(2)}) copy-start(bf16[1,1024,1024]{2,1,0:T(8,128)(2,1)} %param.18) | copy-start | bytes 6291460
  577.0 77.7 %copy-start.17 = (f32[1024,32]{0,1:T(8,128)S(1)}, f32[1024,32]{0,1:T(8,128)}, u32[]{:S(2)}) copy-start(f32[1024,32]{0,1:T(8,128)} %copy-done.16) | copy-start | bytes 393220
  577.0 77.7 %copy-start.21 = (f32[1024,32]{0,1:T(8,128)S(1)}, f32[1024,32]{0,1:T(8,128)}, u32[]{:S(2)}) copy-start(f32[1024,32]{0,1:T(8,128)} %get-tuple-element.169) | copy-start | bytes 393220
  577.0 161.5 %reduce-scatter.31.cloned.1.call-start = ((), (), s32[]{:S(2)}) async-start(), calls=%async_computation.29 | async-start | bytes 786432 | tf_op jit(solution)/shard_map/reduce_scatter | solution.py:294
  580.3 175.6 %reduce-scatter.29.cloned.1.call-start = ((), (), s32[]{:S(2)}) async-start(), calls=%async_computation.28 | async-start | bytes 786432 | tf_op jit(solution)/shard_map/reduce_scatter | solution.py:291
  610.4 162.9 %reduce-scatter.27.cloned.1.call-start = ((), (), s32[]{:S(2)}) async-start(), calls=%async_computation.27 | async-start | bytes 786432 | tf_op jit(solution)/shard_map/reduce_scatter | solution.py:288
  656.2 6.5 copy-start.10
  659.3 131.5 %reduce-scatter.25.cloned.1.call-start = ((), (), s32[]{:S(2)}) async-start(), calls=%async_computation.26 | async-start | bytes 786432 | tf_op jit(solution)/shard_map/reduce_scatter | solution.py:285
  659.4 4.0 copy-start.8
  662.6 1.6 copy-start.6
  662.6 1.6 copy-start.19
  662.6 162.3 %reduce-scatter.23.cloned.1.call-start = ((), (), s32[]{:S(2)}) async-start(), calls=%async_computation.24 | async-start | bytes 2621440 | tf_op jit(solution)/shard_map/reduce_scatter | solution.py:97
  666.4 158.6 %copy-start.12 = (f32[256,1024]{1,0:T(8,128)S(1)}, f32[256,1024]{1,0:T(8,128)}, u32[]{:S(2)}) copy-start(f32[256,1024]{1,0:T(8,128)} %get-tuple-element.147) | copy-start | bytes 3145732
  666.4 161.8 %copy-start.36 = (u32[32]{0:T(128)S(1)}, u32[32]{0:T(128)}, u32[]{:S(2)}) copy-start(u32[32]{0:T(128)} %constant.140) | copy-start | bytes 388
  666.4 163.0 %copy-start.26 = (bf16[1024]{0:T(1024)(128)(2,1)S(1)}, bf16[1024]{0:T(1024)(128)(2,1)}, u32[]{:S(2)}) copy-start(bf16[1024]{0:T(1024)(128)(2,1)} %get-tuple-element.117) | copy-start | bytes 6148
  666.4 163.1 %all-gather.23.cloned.1.call-start = ((), (), s32[]{:S(2)}) async-start(), calls=%async_computation.18 | async-start | bytes 2621440 | tf_op jit(solution)/shard_map/all_gather | solution.py:269
  667.1 282.0 %all-reduce.9.cloned.1.call-start = ((), (), s32[]{:S(2)}) async-start(), calls=%async_computation.33 | async-start | bytes 6291456 | tf_op jit(solution)/shard_map/psum | solution.py:317
  790.8 170.3 %all-gather.29.cloned.1.call-start = ((), (), s32[]{:S(2)}) async-start(), calls=%async_computation.25 | async-start | bytes 2621440 | tf_op jit(solution)/shard_map/all_gather | solution.py:270
  827.0 6.9 copy-start.28
  827.0 6.9 copy-start.27
  949.1 10.3 %copy-start.18 = (bf16[1024,512]{1,0:T(8,128)(2,1)S(1)}, bf16[1024,512]{1,0:T(8,128)(2,1)}, u32[]{:S(2)}) copy-start(bf16[1024,512]{1,0:T(8,128)(2,1)} %get-tuple-element.139) | copy-start | bytes 3145732
Sparse Core Ops, SparseCore 0:
  22.0 47.3 all-gather.30
  71.5 44.4 all-gather.14
  200.9 29.9 reduce-scatter.12
  337.4 22.5 all-gather.24
  408.1 22.5 all-gather.26
  564.1 43.6 reduce-scatter.20
  610.7 42.8 reduce-scatter.18
  656.4 31.0 reduce-scatter.32
  689.8 31.8 reduce-scatter.34
  723.8 14.6 reduce-scatter.30
  741.3 14.6 reduce-scatter.28
  758.6 14.6 reduce-scatter.26
  776.1 14.6 reduce-scatter.24
  793.8 31.1 reduce-scatter.22
  827.7 121.4 all-reduce.8
Sparse Core Ops, SparseCore 1:
  202.8 31.7 all-gather.18
  236.6 22.4 all-gather.16
  260.5 32.9 all-gather.20
  299.5 31.2 reduce-scatter.14
  371.5 31.2 reduce-scatter.16
  669.3 21.6 all-gather.22
  827.1 22.5 all-gather.28
where the time goes:
time: 978 us; the launch traced here: 973 us
  waiting for transfers between devices  529 us (54%)
  matrix products  246 us (25%)
  blocking collectives  86.4 us (9%)
  other arithmetic  78 us (8%)
  between operations  19.7 us (2%)
  local copies, waits for them, and re-layouts  12 us (1%)
    reduce_scatter x4, waiting for transfers between devices, reduce_heads(): lax.psum_scatter(partial_sum.astype(jnp.bfloat16), 'tp', scatter_dimensio...  109 us
    psum x1, waiting for transfers between devices, body(): lax.psum(shares[0].astype(jnp.bfloat16), 'ctx').astype(jnp.float32)  90.2 us
    all_gather x3, waiting for transfers between devices, spread_rows(): return lax.all_gather(rows_low, 'tp', axis=0, tiled=True)  67.4 us
    dot_general x2, matrix products, masked_scores(): jnp.einsum('sqhd,skhd->shqk', queries, key_piece, preferred_element_type=...  49 us
    all_gather x1, waiting for transfers between devices, body(): key_piece = lax.all_gather(keys, 'ctx', axis=1, tiled=True)  46.2 us
    reduce_scatter x1, waiting for transfers between devices, body(): lax.psum_scatter(key_grad_all.astype(jnp.bfloat16), 'ctx', scatter_dimens...  43.1 us
    dot_general x1, matrix products, backward_update(): jnp.einsum('sqhd,skhd->shqk', heads_grad, backward_value_piece, preferred...  41.9 us
    reduce_scatter x1, waiting for transfers between devices, body(): lax.psum_scatter(down_grad.astype(jnp.bfloat16), 'dp', scatter_dimension=...  34.2 us
  transfers between devices with their start and end apart: 22, of which 18 were waited for; matrix products, arithmetic and copies ran while one was open for 8% of the time, Pallas kernels for 0%

commit v1 on v0

--- a/solution.py
+++ b/solution.py
@@ -130,8 +130,11 @@
         jnp.zeros((seqs, heads_here, piece_len), jnp.float32),
         jnp.zeros((seqs, piece_len, heads_here, head_size), jnp.float32),
     )
-    key_piece = lax.all_gather(keys, "ctx", axis=1, tiled=True)
-    value_piece = lax.all_gather(values, "ctx", axis=1, tiled=True)
+    key_piece, value_piece = jnp.split(
+        lax.all_gather(jnp.concatenate([keys, values], axis=0), "ctx", axis=1, tiled=True),
+        [keys.shape[0]],
+        axis=0,
+    )
     needed, doc_keys = touches()
 
     def forward_update(state):

time: 978 us -> 1080 us (1.10)
  waiting for transfers between devices: 529 us -> 626 us
    all_gather x2 -> x3, waiting for transfers between devices: 46.2 us -> 147 us  [the longest x1 57.5 us: body(): lax.all_gather(jnp.concatenate([keys, values], axis=0), 'ctx', axis=1, ti...]
  transfers between devices with their start and end apart: 22 -> 23, of which waited for: 18 -> 20; matrix products, arithmetic and copies ran while one was open for 8% -> 7% of each run, Pallas kernels for 0% -> 0%
where the time goes in v1:
time: 1080 us
  waiting for transfers between devices  626 us (58%)
  matrix products  246 us (23%)
  blocking collectives  86.1 us (8%)
  other arithmetic  82.5 us (8%)
  between operations  19.7 us (2%)
  local copies, waits for them, and re-layouts  13.7 us (1%)
    reduce_scatter x4, waiting for transfers between devices, reduce_heads(): lax.psum_scatter(partial_sum.astype(jnp.bfloat16), 'tp', scatter_dimensio...  108 us
    psum x1, waiting for transfers between devices, body(): lax.psum(shares[0].astype(jnp.bfloat16), 'ctx').astype(jnp.float32)  90.2 us
    all_gather x3, waiting for transfers between devices, spread_rows(): return lax.all_gather(rows_low, 'tp', axis=0, tiled=True)  64.6 us
    all_gather x1, waiting for transfers between devices, body(): lax.all_gather(jnp.concatenate([keys, values], axis=0), 'ctx', axis=1, ti...  57.5 us
    dot_general x2, matrix products, masked_scores(): jnp.einsum('sqhd,skhd->shqk', queries, key_piece, preferred_element_type=...  49.9 us
    all_gather x1, waiting for transfers between devices, body(): backward_key_piece = lax.all_gather(keys, 'ctx', axis=1, tiled=True)  46.5 us
    all_gather x1, waiting for transfers between devices, body(): backward_value_piece = lax.all_gather(values, 'ctx', axis=1, tiled=True)  43.5 us
    reduce_scatter x1, waiting for transfers between devices, body(): lax.psum_scatter(key_grad_all.astype(jnp.bfloat16), 'ctx', scatter_dimens...  43.1 us
  transfers between devices with their start and end apart: 23, of which 20 were waited for; matrix products, arithmetic and copies ran while one was open for 7% of the time, Pallas kernels for 0%

profile of v1, /device:TPU:0, one launch (start us, length us, event | category | flops | bytes accessed | tf_op | source)
XLA Modules:
  0.0 1076.3 jit_solution(5188700071178978599)
XLA Ops:
  8.8 10.2 all_gather.61
  19.0 8.3 all_gather.62
  27.3 7.5 all_gather.63
  35.2 2.3 fusion.96
  37.6 3.5 fusion.81
  41.3 2.4 fusion.78
  47.2 13.2 %all_gather.60 = s32[1,4096]{1,0:T(1,128)S(1)} all-gather(s32[1,1024]{1,0:T(1,128)S(1)} %copy-done.28), channel_id=1, replica_groups=mesh['dp'=2,'ctx'=4,'tp'=4] {'ctx'}, dimensions={1}, use_global_device_ids=true | all-gather | bytes 20480 | tf_op jit(solution)/shard_map/all_gather | solution.py:86
  64.4 7.0 all_gather.65
  71.4 57.5 %all-gather.16.cloned.1.call-done = bf16[2,4096,4,64]{1,3,2,0:T(8,128)(2,1)} async-done(((bf16[2,1024,4,64]{1,3,2,0:T(8,128)(2,1)}), bf16[2,4096,4,64]{1,3,2,0:T(8,128)(2,1)}) %all-gather.16.cloned.1.call-update) | async-done | bytes 4194320 | tf_op jit(solution)/shard_map/all_gather | solution.py:134
  128.9 83.7 %conditional.2 = (f32[1,4,1024]{2,1,0:T(4,128)S(1)}, f32[1,4,1024]{2,1,0:T(4,128)}, f32[1,1024,4,64]{1,3,2,0:T(8,128)S(1)}, f32[1,4,1024]{2,1,0:T(4,128)S(1)}) conditional(s32[]{:T(128)} %convert_element_type.302, () %tuple.32, (s32[1,1024]{1,0:T(1,128)S(1)}, s32[1,4096]{1,0:T(1,128)S(1)}, bf16[1,1024,4,64]{1,3,2,0:T(8,128)(2,1)S(1)}, ...), branch_computations={%region_4.0_spmd, %region_5.8_spmd} | conditional | flops 4483981312 | bytes 224088096 | solution.py:156
  129.1 4.7 broadcast_compare_fusion
  133.8 26.8 %fusion = (f32[4,1024]{1,0:T(4,128)S(1)}, f32[4,1024,4096]{2,1,0:T(8,128)}) fusion(pred[1024,4096]{1,0:T(8,128)(4,1)} %broadcast_compare_fusion, bf16[2,4096,4,64]{1,3,2,0:T(8,128)(2,1)} %get-tuple-element.53, bf16[1,1024,4,64]{1,3,2,0:T(8,128)(2,1)S(1)} %get-tuple-element.52), kind=kOutput, calls=%fused_computation.2 | convolution fusion | flops 2197811200 | bytes 73940992 | tf_op jit(solution)/shard_map/cond/branch_1_fun/sqhd,skhd->shqk/dot_general | solution.py:122
  160.6 23.3 %fusion.2 = f32[4,1024]{1,0:T(4,128)} fusion(f32[4,1024,4096]{2,1,0:T(8,128)} %get-tuple-element.155, f32[4,1024]{1,0:T(4,128)S(1)} %broadcast_maximum_fusion, pred[1024,4096]{1,0:T(8,128)(4,1)} %broadcast_compare_fusion), kind=kLoop, calls=%fused_computation.4 | loop fusion | flops 67104768 | bytes 71335936 | tf_op jit(solution)/shard_map/cond/branch_1_fun/reduce_sum | solution.py:146
  184.7 27.9 %fusion.16 = f32[1,1024,4,64]{1,3,2,0:T(8,128)S(1)} fusion(bf16[2,4096,4,64]{1,3,2,0:T(8,128)(2,1)} %get-tuple-element.53, f32[4,1024,4096]{2,1,0:T(8,128)} %get-tuple-element.155, f32[4,1024]{1,0:T(4,128)S(1)} %broadcast_maximum_fusion, pred[1024,4096]{1,0:T(8,128)(4,1)} %broadcast_compare_fusion, f32[1024,4]{0,1:T(4,128)S(1)} %get-tuple-element.144), kind=kOutput, calls=%fused_computation.14 | convolution fusion | flops 2214854656 | bytes 74481664 | tf_op jit(solution)/shard_map/cond/branch_1_fun/shqk,skhd->sqhd/dot_general | solution.py:147
  216.2 4.4 all-gather.1
  220.6 4.4 all-gather.2
  225.0 20.4 %reduce-scatter.13.cloned.1.call-done = bf16[256,1024]{1,0:T(8,128)(2,1)} async-done(((bf16[1024,1024]{1,0:T(8,128)(2,1)}), bf16[256,1024]{1,0:T(8,128)(2,1)}) %reduce-scatter.13.cloned.1.call-update) | async-done | bytes 524304 | tf_op jit(solution)/shard_map/reduce_scatter | solution.py:97
  248.3 2.3 fusion.115
  251.8 21.8 %all-gather.18.cloned.1.call-done = bf16[1024,1024]{1,0:T(8,128)(2,1)} async-done(((bf16[256,1024]{1,0:T(8,128)(2,1)}), bf16[1024,1024]{1,0:T(8,128)(2,1)}) %all-gather.18.cloned.1.call-update) | async-done | bytes 2097168 | tf_op jit(solution)/shard_map/all_gather | solution.py:102
  273.5 14.3 %fusion.52 = (bf16[1024,1024]{1,0:T(8,128)(2,1)}, f32[1024,1024]{1,0:T(8,128)}) fusion(bf16[1024,1024]{1,0:T(8,128)(2,1)} %all-gather.18.cloned.1.call-done, bf16[1024,1024]{1,0:T(8,128)(2,1)} %all-gather.20.cloned.1.call-done), kind=kOutput, calls=%fused_computation.48 | convolution fusion | flops 2215641088 | bytes 10485760 | tf_op jit(solution)/shard_map/dot_general | solution.py:164
  287.8 20.1 %all-gather.22.cloned.1.call-done = bf16[1024,1024]{1,0:T(8,128)(2,1)} async-done(((bf16[1024,512]{1,0:T(8,128)(2,1)}), bf16[1024,1024]{1,0:T(8,128)(2,1)}) %all-gather.22.cloned.1.call-update) | async-done | bytes 2097168 | tf_op jit(solution)/shard_map/all_gather | solution.py:78
  307.9 5.9 convolution_convert_fusion.3
  314.0 4.4 all-gather.3
  318.4 4.4 all-gather.4
  322.7 22.5 %reduce-scatter.15.cloned.1.call-done = bf16[256,1024]{1,0:T(8,128)(2,1)} async-done(((bf16[1024,1024]{1,0:T(8,128)(2,1)}), bf16[256,1024]{1,0:T(8,128)(2,1)}) %reduce-scatter.15.cloned.1.call-update) | async-done | bytes 524304 | tf_op jit(solution)/shard_map/reduce_scatter | solution.py:97
  349.3 2.5 fusion.122
  351.8 22.7 %all-gather.26.cloned.1.call-done = bf16[1024,1024]{1,0:T(8,128)(2,1)} async-done(((bf16[256,1024]{1,0:T(8,128)(2,1)}), bf16[1024,1024]{1,0:T(8,128)(2,1)}) %all-gather.26.cloned.1.call-update) | async-done | bytes 2097168 | tf_op jit(solution)/shard_map/all_gather | solution.py:102
  374.5 6.3 fusion.58
  382.2 3.7 convolution_convert_fusion.2
  386.2 31.1 %reduce-scatter.17.cloned.1.call-done = bf16[256,1024]{1,0:T(8,128)(2,1)} async-done(((bf16[1024,1024]{1,0:T(8,128)(2,1)}), bf16[256,1024]{1,0:T(8,128)(2,1)}) %reduce-scatter.17.cloned.1.call-update) | async-done | bytes 524304 | tf_op jit(solution)/shard_map/reduce_scatter | solution.py:97
  417.3 2.4 multiply_reduce_fusion
  419.7 2.8 fusion.121
  425.0 20.2 %all-gather.30.cloned.1.call-done = bf16[1024,1024]{1,0:T(8,128)(2,1)} async-done(((bf16[256,1024]{1,0:T(8,128)(2,1)}), bf16[1024,1024]{1,0:T(8,128)(2,1)}) %all-gather.30.cloned.1.call-update) | async-done | bytes 2097168 | tf_op jit(solution)/shard_map/all_gather | solution.py:102
  445.2 2.4 convolution_convert_fusion.6
  449.4 43.5 %all-gather.34.cloned.1.call-done = bf16[4096,4,64]{0,2,1:T(8,128)(2,1)} async-done(((bf16[1024,4,64]{0,2,1:T(8,128)(2,1)}), bf16[4096,4,64]{0,2,1:T(8,128)(2,1)}) %all-gather.34.cloned.1.call-update) | async-done | bytes 2097168 | tf_op jit(solution)/shard_map/all_gather | solution.py:200
  492.9 46.5 %all-gather.28.cloned.1.call-done = bf16[1,4096,4,64]{1,3,2,0:T(8,128)(2,1)} async-done(((bf16[1,1024,4,64]{1,3,2,0:T(8,128)(2,1)}), bf16[1,4096,4,64]{1,3,2,0:T(8,128)(2,1)}) %all-gather.28.cloned.1.call-update) | async-done | bytes 2097168 | tf_op jit(solution)/shard_map/all_gather | solution.py:199
  539.4 129.6 %conditional.3 = (bf16[1,4096,4,64]{1,3,2,0:T(8,128)(2,1)}, bf16[1,4096,4,64]{1,3,2,0:T(8,128)(2,1)}, f32[1,1024,4,32]{1,3,2,0:T(8,128)}, f32[1,1024,4,32]{1,3,2,0:T(8,128)S(1)}) conditional(s32[]{:T(128)} %convert_element_type.302, () %tuple.34, (s32[1,1024]{1,0:T(1,128)S(1)}, s32[1,4096]{1,0:T(1,128)S(1)}, ...), branch_computations={%region_20.21_spmd, %region_21.22_spmd} | conditional | flops 10911748096 | bytes 340906080 | solution.py:231
  539.4 4.7 broadcast_compare_fusion.1
  544.2 23.1 %fusion.36 = f32[4,1024,4096]{2,1,0:T(8,128)} fusion(bf16[1,4096,4,64]{1,3,2,0:T(8,128)(2,1)S(1)} %copy-done.1, bf16[1,1024,4,64]{1,3,2,0:T(8,128)(2,1)S(1)} %get-tuple-element.56), kind=kOutput, calls=%fused_computation.33 | convolution fusion | flops 2147483648 | bytes 69730304 | tf_op jit(solution)/shard_map/cond/branch_1_fun/sqhd,skhd->shqk/dot_general | solution.py:122
  567.3 28.2 %fusion.30 = bf16[1,4096,4,64]{1,3,2,0:T(8,128)(2,1)} fusion(f32[4,1024,4096]{2,1,0:T(8,128)} %fusion.36, f32[4,1024]{1,0:T(4,128)S(1)} %add_bitcast_fusion, pred[1024,4096]{1,0:T(8,128)(4,1)} %broadcast_compare_fusion.1, bf16[1,1024,4,64]{1,3,2,0:T(8,128)(2,1)S(1)} %copy-done.26), kind=kOutput, calls=%fused_computation.29 | convolution fusion | flops 2214592512 | bytes 73940992 | tf_op jit(solution)/shard_map/cond/branch_1_fun/shqk,sqhd->skhd/dot_general | solution.py:206
  595.6 41.7 %multiply_convert_fusion = bf16[4,1024,4096]{2,1,0:T(8,128)(2,1)} fusion(f32[4,1024,4096]{2,1,0:T(8,128)} %fusion.36, f32[4,1024]{1,0:T(4,128)S(1)} %bitcast.240, f32[4,1024]{1,0:T(4,128)S(1)} %add_bitcast_fusion, pred[1024,4096]{1,0:T(8,128)(4,1)} %broadcast_compare_fusion.1, bf16[1,4096,4,64]{1,3,2,0:T(8,128)(2,1)} %get-tuple-element.61, ...), kind=kOutput, calls=%fused_computation.21 | convolution fusion | flops 2248146944 | bytes 107511808 | tf_op jit(solution)/shard_map/cond/branch_1_fun/sqhd,skhd->shqk/dot_general | solution.py:212
  637.2 15.6 %fusion.41 = f32[1,1024,4,64]{1,3,2,0:T(8,128)S(1)} fusion(bf16[4,1024,4096]{2,1,0:T(8,128)(2,1)} %multiply_convert_fusion, bf16[1,4096,4,64]{1,3,2,0:T(8,128)(2,1)S(1)} %copy-done.1), kind=kOutput, calls=%fused_computation.36 | convolution fusion | flops 2147745792 | bytes 36700160 | tf_op jit(solution)/shard_map/cond/branch_1_fun/shqk,skhd->sqhd/dot_general | solution.py:217
  652.8 15.1 %fusion.29 = bf16[1,4096,4,64]{1,3,2,0:T(8,128)(2,1)} fusion(bf16[4,1024,4096]{2,1,0:T(8,128)(2,1)} %multiply_convert_fusion, bf16[1,1024,4,64]{1,3,2,0:T(8,128)(2,1)S(1)} %get-tuple-element.56), kind=kOutput, calls=%fused_computation.28 | convolution fusion | flops 2149580800 | bytes 36175872 | tf_op jit(solution)/shard_map/cond/branch_1_fun/shqk,sqhd->skhd/dot_general | solution.py:226
  670.8 5.3 convolution_convert_fusion.1
  676.2 6.0 convolution_convert_fusion
  682.3 3.3 convolution_convert_fusion.5
  685.6 26.0 %reduce-scatter.21.cloned.1.call-done = bf16[1,1024,4,64]{1,3,2,0:T(8,128)(2,1)} async-done(((bf16[1,4096,4,64]{1,3,2,0:T(8,128)(2,1)}), bf16[1,1024,4,64]{1,3,2,0:T(8,128)(2,1)}) %reduce-scatter.21.cloned.1.call-update) | async-done | bytes 524304 | tf_op jit(solution)/shard_map/reduce_scatter | solution.py:238
  711.6 2.5 fusion.102
  714.2 43.1 %reduce-scatter.19.cloned.1.call-done = bf16[1,1024,4,64]{1,3,2,0:T(8,128)(2,1)} async-done(((bf16[1,4096,4,64]{1,3,2,0:T(8,128)(2,1)}), bf16[1,1024,4,64]{1,3,2,0:T(8,128)(2,1)}) %reduce-scatter.19.cloned.1.call-update) | async-done | bytes 524304 | tf_op jit(solution)/shard_map/reduce_scatter | solution.py:235
  758.5 2.1 multiply_subtract_fusion
  771.4 19.9 %reduce-scatter.33.cloned.1.call-done = bf16[512,1024]{1,0:T(8,128)(2,1)} async-done(((bf16[1024,1024]{1,0:T(8,128)(2,1)}), bf16[512,1024]{1,0:T(8,128)(2,1)}) %reduce-scatter.33.cloned.1.call-update) | async-done | bytes 1048592 | tf_op jit(solution)/shard_map/reduce_scatter | solution.py:300
  791.3 34.0 %reduce-scatter.35.cloned.1.call-done = bf16[1024,512]{1,0:T(8,128)(2,1)} async-done(((bf16[1024,1024]{1,0:T(8,128)(2,1)}), bf16[1024,512]{1,0:T(8,128)(2,1)}) %reduce-scatter.35.cloned.1.call-update) | async-done | bytes 1048592 | tf_op jit(solution)/shard_map/reduce_scatter | solution.py:303
  825.3 16.9 %reduce-scatter.31.cloned.1.call-done = bf16[256,512]{1,0:T(8,128)(2,1)} async-done(((bf16[256,1024]{1,0:T(8,128)(2,1)}), bf16[256,512]{1,0:T(8,128)(2,1)}) %reduce-scatter.31.cloned.1.call-update) | async-done | bytes 262160 | tf_op jit(solution)/shard_map/reduce_scatter | solution.py:297
  842.2 17.3 %reduce-scatter.29.cloned.1.call-done = bf16[512,256]{0,1:T(8,128)(2,1)} async-done(((bf16[1024,256]{0,1:T(8,128)(2,1)}), bf16[512,256]{0,1:T(8,128)(2,1)}) %reduce-scatter.29.cloned.1.call-update) | async-done | bytes 262160 | tf_op jit(solution)/shard_map/reduce_scatter | solution.py:294
  859.6 17.5 %reduce-scatter.27.cloned.1.call-done = bf16[512,256]{0,1:T(8,128)(2,1)} async-done(((bf16[1024,256]{0,1:T(8,128)(2,1)}), bf16[512,256]{0,1:T(8,128)(2,1)}) %reduce-scatter.27.cloned.1.call-update) | async-done | bytes 262160 | tf_op jit(solution)/shard_map/reduce_scatter | solution.py:291
  877.1 17.3 %reduce-scatter.25.cloned.1.call-done = bf16[512,256]{0,1:T(8,128)(2,1)} async-done(((bf16[1024,256]{0,1:T(8,128)(2,1)}), bf16[512,256]{0,1:T(8,128)(2,1)}) %reduce-scatter.25.cloned.1.call-update) | async-done | bytes 262160 | tf_op jit(solution)/shard_map/reduce_scatter | solution.py:288
  894.5 34.1 %reduce-scatter.23.cloned.1.call-done = bf16[256,1024]{1,0:T(8,128)(2,1)} async-done(((bf16[1024,1024]{1,0:T(8,128)(2,1)}), bf16[256,1024]{1,0:T(8,128)(2,1)}) %reduce-scatter.23.cloned.1.call-update) | async-done | bytes 524304 | tf_op jit(solution)/shard_map/reduce_scatter | solution.py:97
  933.1 4.4 bitcast_convert_fusion.1
  937.5 5.3 all_gather.79
  942.9 5.0 all-reduce.6
  948.2 12.0 %all-reduce.4 = (bf16[512]{0:T(512)(128)(2,1)S(1)}, bf16[512]{0:T(512)(128)(2,1)S(1)}, bf16[512]{0:T(512)(128)(2,1)S(1)}, bf16[512]{0:T(512)(128)(2,1)S(1)}) all-reduce(bf16[512]{0:T(512)(128)(2,1)S(1)} %dynamic-slice.3, bf16[512]{0:T(512)(128)(2,1)S(1)} %dynamic-slice.5, ...), channel_id=1, replica_groups=mesh['dp'=2,'ctx'=4,'tp'=4] {'ctx'}, use_global_device_ids=true, to_apply=%region_43.44 | all-reduce | flops 2048 | bytes 8192 | tf_op jit(solution)/shard_map/psum | solution.py:326
  962.6 90.2 %all-reduce.9.cloned.1.call-done = (bf16[512,256]{0,1:T(8,128)(2,1)}, bf16[512,256]{0,1:T(8,128)(2,1)}, bf16[512,256]{0,1:T(8,128)(2,1)}, bf16[256,512]{1,0:T(8,...) async-done(((bf16[512,256]{0,1:T(8,128)(2,1)}, bf16[512,256]{0,1:T(8,128)(2,1)}, bf16[512,256]{0,1:T(8,128)(2,1)}, bf16[256,512]{1,0:T(8,128)(2,1)}, ...) | async-done | bytes 3145744 | tf_op jit(solution)/shard_map/psum | solution.py:320
  1060.3 2.8 convert_element_type.349
  1064.7 4.1 bitcast_convert_fusion
  (200 shorter events, 54.8 us)
Async XLA Ops:
  8.0 120.9 %all-gather.16.cloned.1.call-start = ((), (), s32[]{:S(2)}) async-start(), calls=%async_computation.12 | async-start | bytes 5242880 | tf_op jit(solution)/shard_map/all_gather | solution.py:134
  19.0 22.1 %copy-start.6 = (bf16[1024,256]{1,0:T(8,128)(2,1)}, bf16[1024,256]{1,0:T(8,128)(2,1)S(1)}, u32[]{:S(2)}) copy-start(bf16[1024,256]{1,0:T(8,128)(2,1)S(1)} %all_gather.61) | copy-start | bytes 1572868
  27.3 13.8 %copy-start.4 = (bf16[1024,256]{1,0:T(8,128)(2,1)}, bf16[1024,256]{1,0:T(8,128)(2,1)S(1)}, u32[]{:S(2)}) copy-start(bf16[1024,256]{1,0:T(8,128)(2,1)S(1)} %all_gather.62) | copy-start | bytes 1572868
  34.8 6.3 copy-start.2
  37.6 7.7 copy-start.16
  41.1 3.9 copy-start.23
  43.7 3.4 copy-start.28
  43.7 20.6 %copy-start.27 = (bf16[256,512]{1,0:T(8,128)(2,1)S(1)}, bf16[256,512]{1,0:T(8,128)(2,1)}, u32[]{:S(2)}) copy-start(bf16[256,512]{1,0:T(8,128)(2,1)} %param.24) | copy-start | bytes 786436
  45.0 19.3 %copy-start.20 = (f32[1024,32]{0,1:T(8,128)}, f32[1024,32]{0,1:T(8,128)S(1)}, u32[]{:S(2)}) copy-start(f32[1024,32]{0,1:T(8,128)S(1)} %get-tuple-element.171) | copy-start | bytes 393220
  45.3 0.7 copy-start.10
  47.1 198.3 %reduce-scatter.13.cloned.1.call-start = ((), (), s32[]{:S(2)}) async-start(), calls=%async_computation.13 | async-start | bytes 2621440 | tf_op jit(solution)/shard_map/reduce_scatter | solution.py:97
  71.4 142.0 %copy-start.17 = (bf16[256,1024]{1,0:T(8,128)(2,1)}, bf16[256,1024]{1,0:T(8,128)(2,1)S(1)}, u32[]{:S(2)}) copy-start(bf16[256,1024]{1,0:T(8,128)(2,1)S(1)} %all_gather.65) | copy-start | bytes 1572868
  212.6 3.6 copy-start.32
  212.6 8.0 copy-start.33
  213.5 34.9 %copy-start.14 = (bf16[1,1024,4,64]{1,3,2,0:T(8,128)(2,1)}, bf16[1,1024,4,64]{1,3,2,0:T(8,128)(2,1)S(1)}, u32[]{:S(2)}) copy-start(bf16[1,1024,4,64]{1,3,2,0:T(8,128)(2,1)S(1)} %fusion.116) | copy-start | bytes 1572868
  215.6 36.2 %all-gather.20.cloned.1.call-start = ((), (), s32[]{:S(2)}) async-start(), calls=%async_computation.15 | async-start | bytes 3145728 | tf_op jit(solution)/shard_map/all_gather | solution.py:77
  216.1 57.4 %all-gather.18.cloned.1.call-start = ((), (), s32[]{:S(2)}) async-start(), calls=%async_computation.14 | async-start | bytes 2621440 | tf_op jit(solution)/shard_map/all_gather | solution.py:102
  250.6 57.3 %all-gather.22.cloned.1.call-start = ((), (), s32[]{:S(2)}) async-start(), calls=%async_computation.16 | async-start | bytes 3145728 | tf_op jit(solution)/shard_map/all_gather | solution.py:78
  251.2 94.0 %reduce-scatter.15.cloned.1.call-start = ((), (), s32[]{:S(2)}) async-start(), calls=%async_computation.17 | async-start | bytes 2621440 | tf_op jit(solution)/shard_map/reduce_scatter | solution.py:97
  307.9 6.0 copy-start.34
  307.9 10.4 copy-start.35
  307.9 37.3 %copy-start = (bf16[256,1024]{1,0:T(8,128)(2,1)S(1)}, bf16[256,1024]{1,0:T(8,128)(2,1)}, u32[]{:S(2)}) copy-start(bf16[256,1024]{1,0:T(8,128)(2,1)} %reduce-scatter.13.cloned.1.call-done) | copy-start | bytes 1572868
  313.9 60.6 %all-gather.26.cloned.1.call-start = ((), (), s32[]{:S(2)}) async-start(), calls=%async_computation.19 | async-start | bytes 2621440 | tf_op jit(solution)/shard_map/all_gather | solution.py:102
  351.8 65.5 %reduce-scatter.17.cloned.1.call-start = ((), (), s32[]{:S(2)}) async-start(), calls=%async_computation.20 | async-start | bytes 2621440 | tf_op jit(solution)/shard_map/reduce_scatter | solution.py:97
  374.5 7.7 copy-start.37
  380.8 1.4 copy-start.39
  386.0 59.3 %all-gather.30.cloned.1.call-start = ((), (), s32[]{:S(2)}) async-start(), calls=%async_computation.22 | async-start | bytes 2621440 | tf_op jit(solution)/shard_map/all_gather | solution.py:102
  422.5 70.4 %all-gather.34.cloned.1.call-start = ((), (), s32[]{:S(2)}) async-start(), calls=%async_computation.33 | async-start | bytes 2621440 | tf_op jit(solution)/shard_map/all_gather | solution.py:200
  423.1 116.3 %all-gather.28.cloned.1.call-start = ((), (), s32[]{:S(2)}) async-start(), calls=%async_computation.21 | async-start | bytes 2621440 | tf_op jit(solution)/shard_map/all_gather | solution.py:199
  425.0 286.6 %reduce-scatter.21.cloned.1.call-start = ((), (), s32[]{:S(2)}) async-start(), calls=%async_computation.24 | async-start | bytes 2621440 | tf_op jit(solution)/shard_map/reduce_scatter | solution.py:238
  447.7 0.8 copy-start.25
  539.4 4.8 copy-start.1
  544.2 23.1 %copy-start.26 = (bf16[1,1024,4,64]{1,3,2,0:T(8,128)(2,1)S(1)}, bf16[1,1024,4,64]{1,3,2,0:T(8,128)(2,1)}, u32[]{:S(2)}) copy-start(bf16[1,1024,4,64]{1,3,2,0:T(8,128)(2,1)} %get-tuple-element.60) | copy-start | bytes 1572868 | tf_op jit(solution)/shard_map/cond
  669.0 7.1 copy-start.18
  669.0 1.8 copy-start.36
  669.0 88.3 %reduce-scatter.19.cloned.1.call-start = ((), (), s32[]{:S(2)}) async-start(), calls=%async_computation.23 | async-start | bytes 2621440 | tf_op jit(solution)/shard_map/reduce_scatter | solution.py:235
  669.8 121.5 %reduce-scatter.33.cloned.1.call-start = ((), (), s32[]{:S(2)}) async-start(), calls=%async_computation.31 | async-start | bytes 3145728 | tf_op jit(solution)/shard_map/reduce_scatter | solution.py:300
  676.1 6.1 copy-start.15
  676.1 149.2 %reduce-scatter.35.cloned.1.call-start = ((), (), s32[]{:S(2)}) async-start(), calls=%async_computation.32 | async-start | bytes 3145728 | tf_op jit(solution)/shard_map/reduce_scatter | solution.py:303
  682.2 29.5 %copy-start.8 = (bf16[1,1024,1024]{2,1,0:T(8,128)(2,1)S(1)}, bf16[1,1024,1024]{2,1,0:T(8,128)(2,1)}, u32[]{:S(2)}) copy-start(bf16[1,1024,1024]{2,1,0:T(8,128)(2,1)} %param.18) | copy-start | bytes 6291460
  682.2 76.3 %copy-start.19 = (f32[1,1024,4,32]{1,3,2,0:T(8,128)S(1)}, f32[1,1024,4,32]{1,3,2,0:T(8,128)}, u32[]{:S(2)}) copy-start(f32[1,1024,4,32]{1,3,2,0:T(8,128)} %copy-done.18) | copy-start | bytes 1572868
  682.2 76.3 %copy-start.21 = (f32[1024,32]{0,1:T(8,128)S(1)}, f32[1024,32]{0,1:T(8,128)}, u32[]{:S(2)}) copy-start(f32[1024,32]{0,1:T(8,128)} %copy-done.20) | copy-start | bytes 393220
  682.2 160.0 %reduce-scatter.31.cloned.1.call-start = ((), (), s32[]{:S(2)}) async-start(), calls=%async_computation.30 | async-start | bytes 786432 | tf_op jit(solution)/shard_map/reduce_scatter | solution.py:297
  685.6 174.0 %reduce-scatter.29.cloned.1.call-start = ((), (), s32[]{:S(2)}) async-start(), calls=%async_computation.29 | async-start | bytes 786432 | tf_op jit(solution)/shard_map/reduce_scatter | solution.py:294
  714.2 162.9 %reduce-scatter.27.cloned.1.call-start = ((), (), s32[]{:S(2)}) async-start(), calls=%async_computation.28 | async-start | bytes 786432 | tf_op jit(solution)/shard_map/reduce_scatter | solution.py:291
  760.7 2.6 copy-start.11
  760.7 5.0 copy-start.7
  762.2 132.2 %reduce-scatter.25.cloned.1.call-start = ((), (), s32[]{:S(2)}) async-start(), calls=%async_computation.27 | async-start | bytes 786432 | tf_op jit(solution)/shard_map/reduce_scatter | solution.py:288
  763.3 0.8 copy-start.13
  764.1 3.6 copy-start.5
  765.6 2.1 copy-start.12
  765.6 2.8 copy-start.3
  765.6 2.8 copy-start.24
  765.6 162.9 %reduce-scatter.23.cloned.1.call-start = ((), (), s32[]{:S(2)}) async-start(), calls=%async_computation.25 | async-start | bytes 2621440 | tf_op jit(solution)/shard_map/reduce_scatter | solution.py:97
  770.6 158.0 %copy-start.9 = (f32[256,1024]{1,0:T(8,128)S(1)}, f32[256,1024]{1,0:T(8,128)}, u32[]{:S(2)}) copy-start(f32[256,1024]{1,0:T(8,128)} %get-tuple-element.147) | copy-start | bytes 3145732
  770.6 161.2 %copy-start.38 = (u32[32]{0:T(128)S(1)}, u32[32]{0:T(128)}, u32[]{:S(2)}) copy-start(u32[32]{0:T(128)} %constant.140) | copy-start | bytes 388
  770.6 162.4 %copy-start.29 = (bf16[1024]{0:T(1024)(128)(2,1)S(1)}, bf16[1024]{0:T(1024)(128)(2,1)}, u32[]{:S(2)}) copy-start(bf16[1024]{0:T(1024)(128)(2,1)} %get-tuple-element.117) | copy-start | bytes 6148
  770.6 162.5 %all-gather.24.cloned.1.call-start = ((), (), s32[]{:S(2)}) async-start(), calls=%async_computation.18 | async-start | bytes 2621440 | tf_op jit(solution)/shard_map/all_gather | solution.py:272
  771.3 281.5 %all-reduce.9.cloned.1.call-start = ((), (), s32[]{:S(2)}) async-start(), calls=%async_computation.34 | async-start | bytes 6291456 | tf_op jit(solution)/shard_map/psum | solution.py:320
  894.5 170.3 %all-gather.32.cloned.1.call-start = ((), (), s32[]{:S(2)}) async-start(), calls=%async_computation.26 | async-start | bytes 2621440 | tf_op jit(solution)/shard_map/all_gather | solution.py:273
  930.6 6.9 copy-start.31
  930.6 6.9 copy-start.30
  1052.8 10.3 copy-start.22
Sparse Core Ops, SparseCore 0:
  47.2 81.6 all-gather.15
  215.7 29.6 reduce-scatter.12
  351.9 22.5 all-gather.25
  422.6 22.5 all-gather.29
  447.2 45.6 all-gather.33
  494.9 44.4 all-gather.27
  669.2 42.4 reduce-scatter.20
  714.5 42.8 reduce-scatter.18
  760.2 31.0 reduce-scatter.32
  793.4 31.8 reduce-scatter.34
  827.6 14.6 reduce-scatter.30
  844.9 14.6 reduce-scatter.28
  862.4 14.6 reduce-scatter.26
  879.8 14.6 reduce-scatter.24
  897.4 31.1 reduce-scatter.22
  931.3 121.4 all-reduce.8
Sparse Core Ops, SparseCore 1:
  217.6 31.4 all-gather.19
  251.1 22.4 all-gather.17
  274.9 32.9 all-gather.21
  314.0 31.2 reduce-scatter.14
  386.0 31.2 reduce-scatter.16
  773.5 21.8 all-gather.23
  930.7 22.5 all-gather.31
